TPU v7x, 32 devices: a whole 2x2x4 slice. The times are simulated.
32 devices in a mesh: sup: 16 (over z, y, x), cls: 2 (over core).
Axes of the slice: x: 2, y: 2, z: 4, core: 2. Of those that a mesh axis runs over, the one named last changes fastest.
Arguments:
- support_feats: bfloat16 [512, 8192], P('sup', 'cls'), may hold values from -6 to 6
- target_feats: bfloat16 [128, 8192], P('sup', 'cls'), may hold values from -6 to 6
- scales: bfloat16 [512], replicated, may hold values from 0.5 to 2
- soft_labels: float32 [512, 5376], P('sup', 'cls'), may hold values from -6 to 6
- target_labels: int32 [128], P('sup'), may hold values from 0 to 5375
Outputs:
- predictions: bfloat16 [128, 5376], P('sup', 'cls')
- hypergrad: float32 [512, 5376], P('sup', 'cls')
All inputs are finite; a program needn't handle non-finite values.
Results may differ from a plain program's by a relative error of at most 0.017.
Values may be sent and summed in bfloat16 or wider, within the bound.
No kernel may reach another device: no remote copies, remote signals or barrier semaphores. Data moves between devices by JAX's collectives and lax.ppermute only.
A program may use at most 64 MiB of HBM per device.

v0:
```python
import jax
import jax.numpy as jnp
from jax import lax
from jax.sharding import PartitionSpec as P

F = 8192
ITERS = 2


RIDGE = 0.05
LABEL_SCALE = 16.0


def conjugate(rhs, kernel):
    result = jnp.zeros_like(rhs)
    resid = rhs
    direction = rhs
    norm_now = jnp.sum(resid * resid, axis=0)
    for step in range(ITERS):
        image = jnp.dot(kernel, direction.astype(jnp.bfloat16), preferred_element_type=jnp.float32)
        curve = jnp.sum(direction * image, axis=0)
        step_size = norm_now / curve
        result = result + step_size * direction
        resid = resid - step_size * image
        norm_next = jnp.sum(resid * resid, axis=0)
        direction = resid + norm_next / norm_now * direction
        norm_now = norm_next
    return result


def local(support_feats, target_feats, scales, soft_labels, target_labels):
    own_support = support_feats.shape[0]
    own_targets = target_feats.shape[0]
    class_count = soft_labels.shape[1]
    sup_count = lax.axis_size("sup")
    support_total = own_support * sup_count
    block_rows = own_targets + own_support
    scale_vec = scales.astype(jnp.float32)
    sup_index = lax.axis_index("sup")
    support_first = sup_index * own_support
    local_rows = jnp.concatenate([target_feats, support_feats], axis=0)
    partial_gram = lax.dot_general(
        local_rows,
        lax.all_gather(support_feats, "sup", axis=0, tiled=True),
        (((1,), (1,)), ((), ())),
        preferred_element_type=jnp.float32,
    )
    own_scales = lax.dynamic_slice_in_dim(scale_vec, support_first, own_support)
    factor_all = jnp.concatenate([jnp.ones((own_targets,), jnp.float32), own_scales])
    share = lax.psum_scatter(partial_gram, "cls", scatter_dimension=0, tiled=True)
    first_row = lax.axis_index("cls") * share.shape[0]
    count = share.shape[0]
    rows = first_row + lax.iota(jnp.int32, count)
    factor = lax.dynamic_slice_in_dim(factor_all, first_row, count)
    support_index = support_first + rows - own_targets
    on_diag = (lax.iota(jnp.int32, support_total)[None, :] == support_index[:, None]) & (
        rows >= own_targets
    )[:, None]
    scaled = share * (factor[:, None] * scale_vec[None, :]) / F
    finished = (scaled + jnp.where(on_diag, RIDGE, 0.0)).astype(jnp.bfloat16)
    kernels = lax.all_gather(finished, ("sup", "cls"), axis=0, tiled=True)
    blocks = kernels.reshape(sup_count, block_rows, support_total)
    cross_kernel = blocks[:, :own_targets].reshape(sup_count * own_targets, support_total)
    support_kernel = blocks[:, own_targets:].reshape(support_total, support_total)
    label_cols = lax.all_to_all(soft_labels, "sup", split_axis=1, concat_axis=0, tiled=True)
    col_width = label_cols.shape[1]
    labels_all = lax.all_gather(target_labels, "sup", axis=0, tiled=True)
    columns = (
        lax.axis_index("cls") * class_count + sup_index * col_width + lax.iota(jnp.int32, col_width)
    )
    alpha = conjugate(label_cols, support_kernel)
    predicted = jnp.dot(
        cross_kernel, alpha.astype(jnp.bfloat16), preferred_element_type=jnp.float32
    )
    onehot = (labels_all[:, None] == columns[None, :]).astype(jnp.float32)
    misfit = (predicted - LABEL_SCALE * onehot).astype(jnp.bfloat16)
    rhs = lax.dot_general(
        cross_kernel, misfit, (((0,), (0,)), ((), ())), preferred_element_type=jnp.float32
    )
    hyper_cols = conjugate(rhs, support_kernel)
    predictions = lax.all_to_all(
        predicted.astype(jnp.bfloat16), "sup", split_axis=0, concat_axis=1, tiled=True
    )
    hypergrad = lax.all_to_all(hyper_cols, "sup", split_axis=0, concat_axis=1, tiled=True)
    return (predictions, hypergrad)


def solution(mesh):
    in_specs = (P("sup", "cls"), P("sup", "cls"), P(), P("sup", "cls"), P("sup"))
    out_specs = (P("sup", "cls"), P("sup", "cls"))
    return jax.shard_map(local, mesh=mesh, in_specs=in_specs, out_specs=out_specs, check_vma=False)
```

profile of v0, /device:TPU:0, one launch (start us, length us, event | category | flops | bytes accessed | tf_op | source)
XLA Modules:
  0.0 184.7 jit_solution(661950115012459254)
XLA Ops:
  7.2 0.7 all-gather.3.cloned.1.call-update
  7.9 1.7 all_to_all.42
  9.6 1.1 copy.26
  10.7 8.3 %all-to-all-start = ((f32[32,16,168]{2,0,1:T(8,128)}), f32[32,16,168]{2,0,1:T(8,128)S(1)}, u32[]{:S(2)}, u32[]{:S(2)}) async-start(f32[32,16,168]{2,0,1:T(8,128)} %copy.26), calls=%async_computation | async-start | bytes 1048576 | tf_op jit(solution)/shard_map/all_to_all | solution.py:65
  19.1 0.7 convert_element_type.31
  19.8 0.8 dynamic_slice.6
  20.5 1.2 dynamic-slice.5
  22.4 1.2 dynamic-slice
  24.3 0.9 dynamic-update-slice
  25.2 14.8 %all-reduce.1 = s32[128]{0:T(128)S(1)} all-reduce(s32[128]{0:T(128)S(1)} %dynamic-update-slice), channel_id=1, replica_groups=mesh['sup'=16,'cls'=2] {'sup'}, use_global_device_ids=true, to_apply=%add.1 | all-reduce | flops 128 | bytes 1024
  40.1 52.1 %all-gather.3.cloned.1.call-done = bf16[512,4096]{1,0:T(8,128)(2,1)} async-done(((bf16[32,4096]{1,0:T(8,128)(2,1)}), bf16[512,4096]{1,0:T(8,128)(2,1)}) %all-gather.3.cloned.1.call-update) | async-done | bytes 4194320 | tf_op jit(solution)/shard_map/all_gather | solution.py:44
  92.2 3.6 %fusion.4 = f32[40,512]{1,0:T(8,128)S(1)} fusion(bf16[512,4096]{1,0:T(8,128)(2,1)} %all-gather.3.cloned.1.call-done, bf16[32,4096]{1,0:T(8,128)(2,1)S(1)} %copy-done, bf16[8,4096]{1,0:T(8,128)(2,1)} %param.6), kind=kOutput, calls=%fused_computation.18 | convolution fusion | flops 168427520 | bytes 4603904 | tf_op jit(solution)/shard_map/dot_general | solution.py:42
  95.8 2.9 %fusion = f32[24,512]{1,0:T(8,128)S(1)} fusion(f32[40,512]{1,0:T(8,128)S(1)} %fusion.4), kind=kCustom, calls=%all-reduce-scatter | all-reduce-scatter fusion | flops 24577 | bytes 131584
  98.8 2.3 %collective-permute-start = (f32[4,512]{1,0:T(4,128)S(1)}, f32[4,512]{1,0:T(4,128)S(1)}, u32[]{:S(2)}, u32[]{:S(2)}) collective-permute-start(f32[4,512]{1,0:T(4,128)S(1)} %slice.10), channel_id=1, source_target_pairs={{0,1},{2,3},{4,5},{6,7},{8,9},{10,11},{12,13},{14,15},{16,17},{18,... | collective-permute-start | bytes 24584
  101.3 0.5 collective-permute-done
  102.1 41.4 %all-gather = bf16[32,20,512]{2,1,0:T(8,128)(2,1)S(1)} all-gather(bf16[1,20,512]{2,1,0:T(8,128)(2,1)S(1)} %fusion.29), channel_id=1, replica_groups=mesh['sup'=16,'cls'=2] {'sup','cls'}, dimensions={0}, use_global_device_ids=true | all-gather | bytes 675840 | tf_op jit(solution)/shard_map/all_gather | solution.py:61
  146.5 0.7 copy.31
  147.2 3.5 %all-to-all-start.1 = ((bf16[16,8,168]{2,1,0:T(8,128)(2,1)}), bf16[16,8,168]{2,1,0:T(8,128)(2,1)S(1)}, u32[]{:S(2)}, u32[]{:S(2)}) async-start(bf16[16,8,168]{2,1,0:T(8,128)(2,1)} %bitcast.7), calls=%async_computation.1 | async-start | bytes 131072 | tf_op jit(solution)/shard_map/all_to_all | solution.py:81
  150.9 1.0 copy.33
  151.9 6.3 %all-to-all-done.1 = bf16[16,8,168]{2,1,0:T(8,128)(2,1)S(1)} async-done(((bf16[16,8,168]{2,1,0:T(8,128)(2,1)}), bf16[16,8,168]{2,1,0:T(8,128)(2,1)S(1)}, u32[]{:S(2)}, u32[]{:S(2)}) %all-to-all-start.1) | async-done | bytes 43040 | tf_op jit(solution)/shard_map/all_to_all | solution.py:81
  158.3 3.6 %all-to-all-start.2 = ((f32[16,32,168]{2,1,0:T(8,128)}), f32[16,32,168]{2,1,0:T(8,128)S(1)}, u32[]{:S(2)}, u32[]{:S(2)}) async-start(f32[16,32,168]{2,1,0:T(8,128)} %bitcast.10), calls=%async_computation.2 | async-start | bytes 1048576 | tf_op jit(solution)/shard_map/all_to_all | solution.py:84
  161.9 0.8 all_to_all.49
  162.6 13.9 %all-to-all-done.2 = f32[16,32,168]{2,1,0:T(8,128)S(1)} async-done(((f32[16,32,168]{2,1,0:T(8,128)}), f32[16,32,168]{2,1,0:T(8,128)S(1)}, u32[]{:S(2)}, u32[]{:S(2)}) %all-to-all-start.2) | async-done | bytes 344096 | tf_op jit(solution)/shard_map/all_to_all | solution.py:84
  176.9 1.0 all_to_all.53
  (34 shorter events, 4.2 us)
Async XLA Ops:
  7.2 85.1 %copy-start = (bf16[32,4096]{1,0:T(8,128)(2,1)S(1)}, bf16[32,4096]{1,0:T(8,128)(2,1)}, u32[]{:S(2)}) copy-start(bf16[32,4096]{1,0:T(8,128)(2,1)} %param.5) | copy-start | bytes 786436
  7.2 85.1 %all-gather.3.cloned.1.call-start = ((), (), s32[]{:S(2)}) async-start(), calls=%async_computation.3 | async-start | bytes 4456448 | tf_op jit(solution)/shard_map/all_gather | solution.py:44
  10.7 29.4 %all-to-all-start = ((f32[32,16,168]{2,0,1:T(8,128)}), f32[32,16,168]{2,0,1:T(8,128)S(1)}, u32[]{:S(2)}, u32[]{:S(2)}) async-start(f32[32,16,168]{2,0,1:T(8,128)} %copy.26), calls=%async_computation | async-start | bytes 1048576 | tf_op jit(solution)/shard_map/all_to_all | solution.py:65
  98.8 3.1 %collective-permute-start = (f32[4,512]{1,0:T(4,128)S(1)}, f32[4,512]{1,0:T(4,128)S(1)}, u32[]{:S(2)}, u32[]{:S(2)}) collective-permute-start(f32[4,512]{1,0:T(4,128)S(1)} %slice.10), channel_id=1, source_target_pairs={{0,1},{2,3},{4,5},{6,7},{8,9},{10,11},{12,13},{14,15},{16,17},{18,... | collective-permute-start | bytes 24584
  147.2 11.0 %all-to-all-start.1 = ((bf16[16,8,168]{2,1,0:T(8,128)(2,1)}), bf16[16,8,168]{2,1,0:T(8,128)(2,1)S(1)}, u32[]{:S(2)}, u32[]{:S(2)}) async-start(bf16[16,8,168]{2,1,0:T(8,128)(2,1)} %bitcast.7), calls=%async_computation.1 | async-start | bytes 131072 | tf_op jit(solution)/shard_map/all_to_all | solution.py:81
  158.3 18.3 %all-to-all-start.2 = ((f32[16,32,168]{2,1,0:T(8,128)}), f32[16,32,168]{2,1,0:T(8,128)S(1)}, u32[]{:S(2)}, u32[]{:S(2)}) async-start(f32[16,32,168]{2,1,0:T(8,128)} %bitcast.10), calls=%async_computation.2 | async-start | bytes 1048576 | tf_op jit(solution)/shard_map/all_to_all | solution.py:84
Sparse Core Ops, SparseCore 0:
  10.7 81.4 all-gather.2
where the time goes:
time: 185 us
  waiting for transfers between devices  73.6 us (40%)
  blocking collectives  59.1 us (32%)
  starting transfers between devices  17.7 us (10%)
  between operations  15.5 us (8%)
  local copies, waits for them, and re-layouts  11.3 us (6%)
  matrix products  5.96 us (3%)
    all_gather x1, waiting for transfers between devices, local(): lax.all_gather(support_feats, 'sup', axis=0, tiled=True)  52.1 us
    all_gather x1, blocking collectives, local(): kernels = lax.all_gather(finished, ('sup', 'cls'), axis=0, tiled=True)  41.4 us
    unnamed x2, blocking collectives  17.7 us
    all_to_all x1, waiting for transfers between devices, local(): lax.all_to_all(hyper_cols, 'sup', split_axis=0, concat_axis=1, tiled=True)  13.9 us
    all_to_all x1, starting transfers between devices, local(): lax.all_to_all(soft_labels, 'sup', split_axis=1, concat_axis=0, tiled=True)  8.34 us
    all_to_all x1, waiting for transfers between devices, local(): lax.all_to_all(predicted.astype(jnp.bfloat16), 'sup', split_axis=0, conca...  6.34 us
  transfers between devices with their start and end apart: 5, of which 4 were waited for; matrix products, arithmetic and copies ran while one was open for 4% of the time, Pallas kernels for 0%

commit v1 on v0

v1 whole, which is shorter than its diff:
```python
import functools
import jax
import jax.numpy as jnp
from jax import lax
from jax.experimental import pallas as pl
from jax.experimental.pallas import tpu as pltpu
from jax.sharding import PartitionSpec as P

F = 8192
ITERS = 2


RIDGE = 0.05
LABEL_SCALE = 16.0
T = 128
f32 = jnp.float32
bf16 = jnp.bfloat16
VM = pl.BlockSpec(memory_space=pltpu.VMEM)
SM = pl.BlockSpec(memory_space=pltpu.SMEM)


def conjugate(rhs, kernel):
    resid = rhs
    direction = rhs
    result = None
    norm_now = jnp.sum(resid * resid, axis=0, keepdims=True)
    for step in range(ITERS):
        image = jnp.dot(kernel, direction.astype(bf16), preferred_element_type=f32)
        curve = jnp.sum(direction * image, axis=0, keepdims=True)
        step_size = norm_now / curve
        move = step_size * direction
        result = move if result is None else result + move
        if step + 1 < ITERS:
            resid = resid - step_size * image
            norm_next = jnp.sum(resid * resid, axis=0, keepdims=True)
            direction = resid + norm_next / norm_now * direction
            norm_now = norm_next
    return result


def plain(support_feats, target_feats, scales, soft_labels, target_labels):
    own_support = support_feats.shape[0]
    own_targets = target_feats.shape[0]
    class_count = soft_labels.shape[1]
    sup_count = lax.axis_size("sup")
    support_total = own_support * sup_count
    block_rows = own_targets + own_support
    scale_vec = scales.astype(f32)
    sup_index = lax.axis_index("sup")
    support_first = sup_index * own_support
    local_rows = jnp.concatenate([target_feats, support_feats], axis=0)
    partial_gram = lax.dot_general(
        local_rows,
        lax.all_gather(support_feats, "sup", axis=0, tiled=True),
        (((1,), (1,)), ((), ())),
        preferred_element_type=f32,
    )
    own_scales = lax.dynamic_slice_in_dim(scale_vec, support_first, own_support)
    factor_all = jnp.concatenate([jnp.ones((own_targets,), f32), own_scales])
    share = lax.psum_scatter(partial_gram, "cls", scatter_dimension=0, tiled=True)
    first_row = lax.axis_index("cls") * share.shape[0]
    count = share.shape[0]
    rows = first_row + lax.iota(jnp.int32, count)
    factor = lax.dynamic_slice_in_dim(factor_all, first_row, count)
    support_index = support_first + rows - own_targets
    on_diag = (lax.iota(jnp.int32, support_total)[None, :] == support_index[:, None]) & (
        rows >= own_targets
    )[:, None]
    scaled = share * (factor[:, None] * scale_vec[None, :]) / F
    finished = (scaled + jnp.where(on_diag, RIDGE, 0.0)).astype(bf16)
    kernels = lax.all_gather(finished, ("sup", "cls"), axis=0, tiled=True)
    blocks = kernels.reshape(sup_count, block_rows, support_total)
    cross_kernel = blocks[:, :own_targets].reshape(sup_count * own_targets, support_total)
    support_kernel = blocks[:, own_targets:].reshape(support_total, support_total)
    label_cols = lax.all_to_all(soft_labels, "sup", split_axis=1, concat_axis=0, tiled=True)
    col_width = label_cols.shape[1]
    labels_all = lax.all_gather(target_labels, "sup", axis=0, tiled=True)
    columns = (
        lax.axis_index("cls") * class_count + sup_index * col_width + lax.iota(jnp.int32, col_width)
    )
    alpha = conjugate(label_cols, support_kernel)
    predicted = jnp.dot(cross_kernel, alpha.astype(bf16), preferred_element_type=f32)
    onehot = (labels_all[:, None] == columns[None, :]).astype(f32)
    misfit = (predicted - LABEL_SCALE * onehot).astype(bf16)
    rhs = lax.dot_general(
        cross_kernel, misfit, (((0,), (0,)), ((), ())), preferred_element_type=f32
    )
    hyper_cols = conjugate(rhs, support_kernel)
    predictions = lax.all_to_all(
        predicted.astype(bf16), "sup", split_axis=0, concat_axis=1, tiled=True
    )
    hypergrad = lax.all_to_all(hyper_cols, "sup", split_axis=0, concat_axis=1, tiled=True)
    return (predictions, hypergrad)


def halves(blocks):
    cols = [[(i, j) for i in range(j, blocks + 1)] for j in range(blocks)]
    first, second = [], []
    for j, col in enumerate(cols):
        (first if j % 4 in (0, 3) else second).extend(col)
    return first, second


def pack_labels(ns, x_ref, t_ref, o_ref):
    own = x_ref.shape[0]
    rem = x_ref.shape[1] // ns - T
    half = own // 2
    for s in range(ns):
        o_ref[s, 0:own, :] = x_ref[:, s * T : (s + 1) * T]
        a = ns * T + s * rem
        o_ref[s, own : own + half, 0:rem] = x_ref[0:half, a : a + rem]
        o_ref[s, own : own + half, rem : 2 * rem] = x_ref[half:own, a : a + rem]
        o_ref[s, own : own + half, 2 * rem : T] = t_ref[:, 2 * rem : T]


def gram(ns, own_support, c_ref, a_ref, b_ref, o_ref, x_ref):
    width = a_ref.shape[2]
    total = ns * own_support
    for s in range(ns):
        r = slice(s * own_support, (s + 1) * own_support)
        x_ref[r, 0:width] = a_ref[s, 0:own_support]
        x_ref[r, width : 2 * width] = b_ref[s, 0:own_support]
    tgt = a_ref.shape[1] - own_support
    nt = ns * tgt
    x_ref[total : total + nt, 0:width] = a_ref[:, own_support:, :].reshape(nt, width)
    x_ref[total : total + nt, width : 2 * width] = b_ref[:, own_support:, :].reshape(nt, width)
    blocks = total // T
    rows_all = total + nt
    for half in range(2):
        @pl.when(c_ref[0] == half)
        def _():
            off = 0
            for j in range(blocks):
                if (j % 4 in (0, 3)) != (half == 0):
                    continue
                n = rows_all - j * T
                o_ref[off : off + n, :] = lax.dot_general(
                    x_ref[j * T :, :],
                    x_ref[j * T : (j + 1) * T, :],
                    (((1,), (1,)), ((), ())),
                    preferred_element_type=f32,
                )
                off += n


def finish(ns, p_ref, f_ref, d_ref, o_ref):
    total = p_ref[0]
    for s in range(1, ns):
        total = total + p_ref[s]
    done = (total * f_ref[...] + d_ref[...]).astype(bf16)
    for s in range(ns):
        o_ref[s] = done


def solve(ns, own, tgt, rem, c_ref, own_ref, oth_ref, lab_ref, o_ref, k_ref, g_ref):
    total = ns * own
    nt = ns * tgt
    blocks = total // T
    tables = halves(blocks)
    core = c_ref[0]
    for half in range(2):
        @pl.when(core == half)
        def _():
            for ref, table in ((own_ref, tables[half]), (oth_ref, tables[1 - half])):
                for m, (i, j) in enumerate(table):
                    block = ref[m * T : (m + 1) * T, :]
                    cols = slice(j * T, (j + 1) * T)
                    if i == blocks:
                        g_ref[:, cols] = block
                    else:
                        rows = slice(i * T, (i + 1) * T)
                        k_ref[rows, cols] = block
                        if i != j:
                            k_ref[cols, rows] = block.T
    half = own // 2
    main = lab_ref[:, 0:own, :].reshape(total, T)
    spill = lab_ref[:, own : own + half, :]
    moved = pltpu.roll(spill.reshape(ns * half, T), T - rem, 1).reshape(ns, half, T)
    extra = jnp.concatenate([spill, moved], axis=1).reshape(total, T)
    b = jnp.concatenate([main, extra], axis=1)
    kernel = k_ref[...]
    cross = g_ref[...]
    alpha = conjugate(b, kernel)
    predicted = jnp.dot(cross, alpha.astype(bf16), preferred_element_type=f32)
    lane = lax.broadcasted_iota(jnp.int32, (nt, 2 * T), 1)
    columns = jnp.where(lane < T, lane + c_ref[1], lane + c_ref[2]).astype(f32)
    classes = lab_ref[:, own : own + tgt, T - 1 : T].reshape(nt, 1)
    onehot = jnp.where(columns == classes, LABEL_SCALE, 0.0)
    misfit = (predicted - onehot).astype(bf16)
    rhs = lax.dot_general(cross, misfit, (((0,), (0,)), ((), ())), preferred_element_type=f32)
    hyper = conjugate(rhs, kernel).astype(bf16)
    low = predicted.astype(bf16)
    o_ref[:, 0:own, :] = hyper[:, 0:T].reshape(ns, own, T)
    o_ref[:, own : own + tgt, :] = low[:, 0:T].reshape(ns, tgt, T)
    tail = hyper[:, T : T + rem].reshape(ns, own, rem)
    o_ref[:, own + tgt :, 0:rem] = tail[:, 0:half]
    o_ref[:, own + tgt :, rem : 2 * rem] = tail[:, half:own]
    o_ref[:, own + tgt : own + 2 * tgt, 2 * rem : 3 * rem] = low[:, T : T + rem].reshape(ns, tgt, rem)


def unpack(ns, own, tgt, rem, x_ref, p_ref, h_ref):
    half = own // 2
    for s in range(ns):
        cols = slice(s * T, (s + 1) * T)
        h_ref[:, cols] = x_ref[s, 0:own].astype(f32)
        p_ref[:, cols] = x_ref[s, own : own + tgt]
        a = ns * T + s * rem
        tail = x_ref[s, own + tgt :].astype(f32)
        h_ref[0:half, a : a + rem] = tail[:, 0:rem]
        h_ref[half:own, a : a + rem] = tail[:, rem : 2 * rem]
        p_ref[:, a : a + rem] = tail[0:tgt, 2 * rem : 3 * rem].astype(bf16)


def packed(support_feats, target_feats, scales, soft_labels, target_labels):
    own, width = support_feats.shape
    tgt = target_feats.shape[0]
    ns = lax.axis_size("sup")
    total = own * ns
    blocks = total // T
    class_count = soft_labels.shape[1]
    rem = class_count // ns - T
    sup = lax.axis_index("sup")
    core = lax.axis_index("cls")
    scale_vec = scales.astype(f32)
    fb = width // ns

    rows = jnp.concatenate([support_feats, target_feats], axis=0)
    feats = rows.reshape(own + tgt, ns, fb).transpose(1, 0, 2)
    feats = lax.all_to_all(feats, "sup", 0, 0)

    half = own // 2
    classes = jnp.pad(target_labels.astype(f32), (0, half - tgt))
    classes = jnp.broadcast_to(classes[:, None], (half, T))
    labels = pl.pallas_call(
        functools.partial(pack_labels, ns),
        out_shape=jax.ShapeDtypeStruct((ns, own + half, T), f32),
        in_specs=[VM, VM],
        out_specs=VM,
    )(soft_labels, classes)
    labels = lax.all_to_all(labels, "sup", 0, 0)

    first, second = halves(blocks)
    count = len(first) * T
    chunk = count // ns
    by_block = scale_vec.reshape(blocks, T)
    row_scale = jnp.concatenate([by_block, jnp.ones((1, T), f32)])
    order = first + second
    left = jnp.concatenate([row_scale[i] for i, _ in order])
    mine = core * count + sup * chunk
    left = lax.dynamic_slice_in_dim(left, mine, chunk)
    spot = mine + lax.iota(jnp.int32, chunk)
    which = spot // T
    right = jnp.stack([by_block[j] for _, j in order])
    right = right[which]
    factor = left[:, None] * right / F
    on_diag = jnp.array([i == j for i, j in order])[which]
    diag = jnp.where(
        on_diag[:, None] & (lax.iota(jnp.int32, T)[None, :] == (spot % T)[:, None]), RIDGE, 0.0
    ).astype(f32)

    swap = [(0, 1), (1, 0)]
    other = lax.ppermute(feats, "cls", swap)
    info = jnp.stack(
        [core, core * class_count + sup * T, core * class_count + ns * T + sup * rem - T]
    ).astype(jnp.int32)
    partial = pl.pallas_call(
        functools.partial(gram, ns, own),
        out_shape=jax.ShapeDtypeStruct((count, T), f32),
        in_specs=[SM, VM, VM],
        out_specs=VM,
        scratch_shapes=[pltpu.VMEM((total + ns * tgt, 2 * fb), bf16)],
    )(info, feats, other)
    partial = lax.all_to_all(partial.reshape(ns, chunk, T), "sup", 0, 0)
    done = pl.pallas_call(
        functools.partial(finish, ns),
        out_shape=jax.ShapeDtypeStruct((ns, chunk, T), bf16),
        in_specs=[VM, VM, VM],
        out_specs=VM,
    )(partial, factor, diag)
    done = lax.all_to_all(done, "sup", 0, 0).reshape(count, T)
    done_other = lax.ppermute(done, "cls", swap)
    result = pl.pallas_call(
        functools.partial(solve, ns, own, tgt, rem),
        out_shape=jax.ShapeDtypeStruct((ns, own + tgt + half, T), bf16),
        in_specs=[SM, VM, VM, VM],
        out_specs=VM,
        scratch_shapes=[pltpu.VMEM((total, total), bf16), pltpu.VMEM((ns * tgt, total), bf16)],
    )(info, done, done_other, labels)
    result = lax.all_to_all(result, "sup", 0, 0)
    return tuple(
        pl.pallas_call(
            functools.partial(unpack, ns, own, tgt, rem),
            out_shape=(
                jax.ShapeDtypeStruct((tgt, class_count), bf16),
                jax.ShapeDtypeStruct((own, class_count), f32),
            ),
            in_specs=[VM],
            out_specs=(VM, VM),
        )(result)
    )


def fits(mesh, args):
    ns, nc = mesh.shape["sup"], mesh.shape["cls"]
    total, feats = args[0].shape
    nt = args[1].shape[0]
    classes = args[3].shape[1]
    if nc != 2 or total % T or nt != T or (total // T) % 4 or total % (32 * ns):
        return False
    own, tgt, width = total // ns, nt // ns, classes // (nc * ns)
    first, second = halves(total // T)
    return (
        own == 32
        and tgt == 8
        and len(first) == len(second)
        and len(first) * T % (8 * ns) == 0
        and feats % (nc * ns * T) == 0
        and T < width <= T + T // 3
        and width % 8 == 0
    )


def solution(mesh):
    in_specs = (P("sup", "cls"), P("sup", "cls"), P(), P("sup", "cls"), P("sup"))
    out_specs = (P("sup", "cls"), P("sup", "cls"))

    def run(*args):
        body = packed if fits(mesh, args) else plain
        return jax.shard_map(
            body, mesh=mesh, in_specs=in_specs, out_specs=out_specs, check_vma=False
        )(*args)

    return run
```

time: 185 us -> 96.3 us (0.52)
  blocking collectives: 59.1 us -> 12.5 us
  waiting for transfers between devices: 73.6 us -> 41.2 us
  between operations: 15.5 us -> 0.8 us
  Pallas kernels: 0 us -> 12.3 us
  matrix products: 5.96 us -> 0 us
  local copies, waits for them, and re-layouts: 11.3 us -> 6.57 us
  starting transfers between devices: 17.7 us -> 19.7 us
    all_gather x1 -> x0, waiting for transfers between devices: 52.1 us -> none  [local(): lax.all_gather(support_feats, 'sup', axis=0, tiled=True)]
    all_gather x1 -> x0, blocking collectives: 41.4 us -> none  [local(): kernels = lax.all_gather(finished, ('sup', 'cls'), axis=0, tiled=True)]
    all_to_all x3 -> x4, waiting for transfers between devices: 20.3 us -> 40.2 us  [the longest x1 12 us: packed(): partial = lax.all_to_all(partial.reshape(ns, chunk, T), 'sup', 0, 0)]
    unnamed x2 -> x0, blocking collectives: 17.7 us -> none
    all_to_all x0 -> x1, blocking collectives: none -> 12.5 us  [packed(): result = lax.all_to_all(result, 'sup', 0, 0)]
    pallas_call x0 -> x5, Pallas kernels: none -> 12.3 us  [the longest x1 4.63 us: packed(): pl.pallas_call(functools.partial(solve, ns, own, tgt, rem), out_shape=jax...]
    dot_general x7 -> x0, matrix products: 5.96 us -> none  [the longest x1 3.59 us: local(): lax.dot_general(local_rows, lax.all_gather(support_feats, 'sup', axis=0,...]
    all_to_all x7 -> x0, local copies, waits for them, and re-layouts: 5.1 us -> none  [the longest x3 2.98 us: local(): lax.all_to_all(soft_labels, 'sup', split_axis=1, concat_axis=0, tiled=True)]
  transfers between devices with their start and end apart: 5 -> 6, of which waited for: 4 -> 5; matrix products, arithmetic and copies ran while one was open for 4% -> 4% of each run, Pallas kernels for 0% -> 2%
where the time goes in v1:
time: 96.3 us; the launch traced here: 95.6 us
  waiting for transfers between devices  41.2 us (43%)
  starting transfers between devices  19.7 us (20%)
  blocking collectives  12.5 us (13%)
  Pallas kernels  12.3 us (13%)
  local copies, waits for them, and re-layouts  6.57 us (7%)
  other arithmetic  2.39 us (2%)
    all_to_all x1, blocking collectives, packed(): result = lax.all_to_all(result, 'sup', 0, 0)  12.5 us
    all_to_all x1, waiting for transfers between devices, packed(): partial = lax.all_to_all(partial.reshape(ns, chunk, T), 'sup', 0, 0)  12 us
    all_to_all x1, waiting for transfers between devices, packed(): labels = lax.all_to_all(labels, 'sup', 0, 0)  11.9 us
    all_to_all x1, waiting for transfers between devices, packed(): feats = lax.all_to_all(feats, 'sup', 0, 0)  10.6 us
    all_to_all x1, starting transfers between devices, packed(): feats = lax.all_to_all(feats, 'sup', 0, 0)  8.34 us
    all_to_all x1, waiting for transfers between devices, packed(): done = lax.all_to_all(done, 'sup', 0, 0).reshape(count, T)  5.76 us
    pallas_call x1, Pallas kernels, packed(): pl.pallas_call(functools.partial(solve, ns, own, tgt, rem), out_shape=jax...  4.63 us
    all_to_all x1, starting transfers between devices, packed(): done = lax.all_to_all(done, 'sup', 0, 0).reshape(count, T)  3.95 us
  transfers between devices with their start and end apart: 6, of which 5 were waited for; matrix products, arithmetic and copies ran while one was open for 4% of the time, Pallas kernels for 2%

profile of v1, /device:TPU:0, one launch (start us, length us, event | category | flops | bytes accessed | tf_op | source)
XLA Modules:
  0.0 95.6 jit_solution(16234788147119448697)
XLA Ops:
  0.6 1.0 %pad_maximum_fusion = bf16[40,4096]{1,0:T(8,128)(2,1)S(1)} fusion(bf16[8,4096]{1,0:T(8,128)(2,1)} %param.7, bf16[32,4096]{1,0:T(8,128)(2,1)} %param.6), kind=kLoop, calls=%fused_computation.3 | loop fusion | flops 655360 | bytes 655360 | tf_op jit(solution)/shard_map/concatenate | solution.py:227
  1.6 0.7 copy.11
  2.4 8.3 %all-to-all-start = ((bf16[16,40,256]{2,1,0:T(8,128)(2,1)}), bf16[16,40,256]{2,1,0:T(8,128)(2,1)S(1)}, u32[]{:S(2)}, u32[]{:S(2)}) async-start(bf16[16,40,256]{2,1,0:T(8,128)(2,1)} %bitcast.21), calls=%async_computation | async-start | bytes 655360 | tf_op jit(solution)/shard_map/all_to_all | solution.py:229
  11.5 10.6 %all-to-all-done.a_ref = bf16[16,40,256]{2,1,0:T(8,128)(2,1)S(1)} async-done(((bf16[16,40,256]{2,1,0:T(8,128)(2,1)}), bf16[16,40,256]{2,1,0:T(8,128)(2,1)S(1)}, u32[]{:S(2)}, u32[]{:S(2)}) %all-to-all-start) | async-done | bytes 327712 | tf_op jit(solution)/shard_map/all_to_all | solution.py:229
  22.7 1.0 %collective-permute-done.b_ref = bf16[16,40,256]{2,1,0:T(8,128)(2,1)S(1)} collective-permute-done((bf16[16,40,256]{2,1,0:T(8,128)(2,1)S(1)}, bf16[16,40,256]{2,1,0:T(8,128)(2,1)S(1)}, u32[]{:S(2)}, u32[]{:S(2)}) %collective-permute-start) | collective-permute-done | bytes 327712 | tf_op jit(solution)/shard_map/ppermute | solution.py:262
  23.7 0.7 copy-done.5
  24.4 2.3 %shard_map.77 = f32[896,128]{1,0:T(8,128)} custom-call(s32[3]{0:T(128)} %pad_add_fusion.c_ref, bf16[16,40,256]{2,1,0:T(8,128)(2,1)} %copy-done.3, bf16[16,40,256]{2,1,0:T(8,128)(2,1)} %copy-done.5), custom_call_target="tpu_custom_call" | custom-call | tf_op jit(solution)/shard_map/pallas_call | solution.py:266
  26.7 3.7 %all-to-all-start.1 = ((f32[16,56,128]{2,1,0:T(8,128)}), f32[16,56,128]{2,1,0:T(8,128)S(1)}, u32[]{:S(2)}, u32[]{:S(2)}) async-start(f32[16,56,128]{2,1,0:T(8,128)} %bitcast.22), calls=%async_computation.1 | async-start | bytes 917504 | tf_op jit(solution)/shard_map/all_to_all | solution.py:273
  30.4 0.8 gather_fusion.1
  32.0 0.7 multiply_multiply_fusion
  32.7 12.0 %all-to-all-done.1.p_ref = f32[16,56,128]{2,1,0:T(8,128)S(1)} async-done(((f32[16,56,128]{2,1,0:T(8,128)}), f32[16,56,128]{2,1,0:T(8,128)S(1)}, u32[]{:S(2)}, u32[]{:S(2)}) %all-to-all-start.1) | async-done | bytes 458784 | tf_op jit(solution)/shard_map/all_to_all | solution.py:273
  44.7 0.8 copy-done.1
  45.5 1.8 %shard_map.78 = bf16[16,56,128]{2,1,0:T(8,128)(2,1)} custom-call(f32[16,56,128]{2,1,0:T(8,128)} %copy-done.1, f32[56,128]{1,0:T(8,128)} %get-tuple-element.7.f_ref, f32[56,128]{1,0:T(8,128)} %get-tuple-element.8.d_ref), custom_call_target="tpu_custom_call" | custom-call | tf_op jit(solution)/shard_map/pallas_call | solution.py:274
  47.2 4.0 %all-to-all-start.2 = ((bf16[16,56,128]{2,1,0:T(8,128)(2,1)}), bf16[16,56,128]{2,1,0:T(8,128)(2,1)S(1)}, u32[]{:S(2)}, u32[]{:S(2)}) async-start(bf16[16,56,128]{2,1,0:T(8,128)(2,1)} %shard_map.78), calls=%async_computation.2 | async-start | bytes 458752 | tf_op jit(solution)/shard_map/all_to_all | solution.py:280
  51.2 0.7 broadcast_in_dim.10.t_ref
  51.9 1.9 %shard_map.79 = f32[16,48,128]{2,1,0:T(8,128)} custom-call(f32[32,2688]{1,0:T(8,128)} %x_ref.1, f32[16,128]{1,0:T(8,128)} %broadcast_in_dim.10.t_ref), custom_call_target="tpu_custom_call" | custom-call | tf_op jit(solution)/shard_map/pallas_call | solution.py:234
  53.8 5.8 %all-to-all-done.2 = bf16[16,56,128]{2,1,0:T(8,128)(2,1)S(1)} async-done(((bf16[16,56,128]{2,1,0:T(8,128)(2,1)}), bf16[16,56,128]{2,1,0:T(8,128)(2,1)S(1)}, u32[]{:S(2)}, u32[]{:S(2)}) %all-to-all-start.2) | async-done | bytes 229408 | tf_op jit(solution)/shard_map/all_to_all | solution.py:280
  59.6 3.7 %all-to-all-start.3 = ((f32[16,48,128]{2,1,0:T(8,128)}), f32[16,48,128]{2,1,0:T(8,128)S(1)}, u32[]{:S(2)}, u32[]{:S(2)}) async-start(f32[16,48,128]{2,1,0:T(8,128)} %shard_map.79), calls=%async_computation.3 | async-start | bytes 786432 | tf_op jit(solution)/shard_map/all_to_all | solution.py:240
  63.3 11.9 %all-to-all-done.3.lab_ref = f32[16,48,128]{2,1,0:T(8,128)S(1)} async-done(((f32[16,48,128]{2,1,0:T(8,128)}), f32[16,48,128]{2,1,0:T(8,128)S(1)}, u32[]{:S(2)}, u32[]{:S(2)}) %all-to-all-start.3) | async-done | bytes 393248 | tf_op jit(solution)/shard_map/all_to_all | solution.py:240
  75.2 0.7 copy-done.2
  76.0 0.7 copy-done.6
  76.6 4.6 %shard_map.80 = bf16[16,56,128]{2,1,0:T(8,128)(2,1)} custom-call(s32[3]{0:T(128)} %pad_add_fusion.c_ref, bf16[896,128]{1,0:T(8,128)(2,1)} %bitcast.25, bf16[896,128]{1,0:T(8,128)(2,1)} %copy-done.6, f32[16,48,128]{2,1,0:T(8,128)} %copy-done.2), custom_call_target="tpu_custom_call" | custom-call | tf_op jit(solution)/shard_map/pallas_call | solution.py:282
  81.3 12.5 %all_to_all.25.x_ref = bf16[16,56,128]{2,1,0:T(8,128)(2,1)} all-to-all(bf16[16,56,128]{2,1,0:T(8,128)(2,1)} %shard_map.80), channel_id=1, replica_groups=mesh['sup'=16,'cls'=2] {'sup'}, dimensions={0} | all-to-all | bytes 458752 | tf_op jit(solution)/shard_map/all_to_all | solution.py:289
  93.8 1.8 %shard_map.81 = (bf16[8,2688]{1,0:T(8,128)(2,1)}, f32[32,2688]{1,0:T(8,128)}) custom-call(bf16[16,56,128]{2,1,0:T(8,128)(2,1)} %all_to_all.25.x_ref), custom_call_target="tpu_custom_call" | custom-call | tf_op jit(solution)/shard_map/pallas_call | solution.py:291
  (36 shorter events, 2.2 us)
Async XLA Ops:
  2.4 19.7 %all-to-all-start = ((bf16[16,40,256]{2,1,0:T(8,128)(2,1)}), bf16[16,40,256]{2,1,0:T(8,128)(2,1)S(1)}, u32[]{:S(2)}, u32[]{:S(2)}) async-start(bf16[16,40,256]{2,1,0:T(8,128)(2,1)} %bitcast.21), calls=%async_computation | async-start | bytes 655360 | tf_op jit(solution)/shard_map/all_to_all | solution.py:229
  10.7 0.7 copy-start.7
  22.1 1.6 %copy-start.3 = (bf16[16,40,256]{2,1,0:T(8,128)(2,1)}, bf16[16,40,256]{2,1,0:T(8,128)(2,1)S(1)}, u32[]{:S(2)}) copy-start(bf16[16,40,256]{2,1,0:T(8,128)(2,1)S(1)} %all-to-all-done.a_ref) | copy-start | bytes 983044
  22.1 1.6 %collective-permute-start = (bf16[16,40,256]{2,1,0:T(8,128)(2,1)S(1)}, bf16[16,40,256]{2,1,0:T(8,128)(2,1)S(1)}, u32[]{:S(2)}, u32[]{:S(2)}) collective-permute-start(bf16[16,40,256]{2,1,0:T(8,128)(2,1)S(1)} %all-to-all-done.a_ref), channel_id=1, source_target_pairs={{0,1},{1,0},{2,3},{3,2},{4,5},{5,4},{6,7},{7,6},{8,9},{9,8},{10,11... | collective-permute-start | bytes 983048 | tf_op jit(solution)/shard_map/ppermute | solution.py:262
  23.7 0.7 copy-start.5
  26.7 3.7 %copy-start = (pred[14]{0:T(512)(128)(4,1)S(1)}, pred[14]{0:T(512)(128)(4,1)}, u32[]{:S(2)}) copy-start(pred[14]{0:T(512)(128)(4,1)} %constant.66.clone) | copy-start | bytes 46
  26.7 18.0 %all-to-all-start.1 = ((f32[16,56,128]{2,1,0:T(8,128)}), f32[16,56,128]{2,1,0:T(8,128)S(1)}, u32[]{:S(2)}, u32[]{:S(2)}) async-start(f32[16,56,128]{2,1,0:T(8,128)} %bitcast.22), calls=%async_computation.1 | async-start | bytes 917504 | tf_op jit(solution)/shard_map/all_to_all | solution.py:273
  44.7 0.8 copy-start.1
  47.2 4.0 %copy-start.8 = (s32[8]{0:T(128)S(1)}, s32[8]{0:T(128)}, u32[]{:S(2)}) copy-start(s32[8]{0:T(128)} %param.10) | copy-start | bytes 100
  47.2 12.3 %all-to-all-start.2 = ((bf16[16,56,128]{2,1,0:T(8,128)(2,1)}), bf16[16,56,128]{2,1,0:T(8,128)(2,1)S(1)}, u32[]{:S(2)}, u32[]{:S(2)}) async-start(bf16[16,56,128]{2,1,0:T(8,128)(2,1)} %shard_map.78), calls=%async_computation.2 | async-start | bytes 458752 | tf_op jit(solution)/shard_map/all_to_all | solution.py:280
  59.5 3.7 %copy-start.4 = (bf16[16,56,128]{2,1,0:T(8,128)(2,1)}, bf16[16,56,128]{2,1,0:T(8,128)(2,1)S(1)}, u32[]{:S(2)}) copy-start(bf16[16,56,128]{2,1,0:T(8,128)(2,1)S(1)} %all-to-all-done.2) | copy-start | bytes 688132
  59.6 15.7 %all-to-all-start.3 = ((f32[16,48,128]{2,1,0:T(8,128)}), f32[16,48,128]{2,1,0:T(8,128)S(1)}, u32[]{:S(2)}, u32[]{:S(2)}) async-start(f32[16,48,128]{2,1,0:T(8,128)} %shard_map.79), calls=%async_computation.3 | async-start | bytes 786432 | tf_op jit(solution)/shard_map/all_to_all | solution.py:240
  63.2 12.0 %collective-permute-start.1 = (bf16[896,128]{1,0:T(8,128)(2,1)S(1)}, bf16[896,128]{1,0:T(8,128)(2,1)S(1)}, u32[]{:S(2)}, u32[]{:S(2)}) collective-permute-start(bf16[896,128]{1,0:T(8,128)(2,1)S(1)} %bitcast.24), channel_id=1, source_target_pairs={{0,1},{1,0},{2,3},{3,2},{4,5},{5,4},{6,7},{7,6},{8,9},{9,8},{10,11... | collective-permute-start | bytes 688136 | tf_op jit(solution)/shard_map/ppermute | solution.py:281
  75.2 0.8 copy-start.2
  76.0 0.7 copy-start.6
